TPU v7x, 32 devices: a whole 2x2x4 slice. The times are simulated.
32 devices in a mesh: row: 8 (over y, x, core), col: 4 (over z).
Axes of the slice: x: 2, y: 2, z: 4, core: 2. Of those that a mesh axis runs over, the one named last changes fastest.
Arguments:
- final_amp: bfloat16 [8, 32, 128, 440], P('row', 'col'), may hold values from -0.19921875 to 0.19921875
- initial_amp: bfloat16 [4, 32, 128, 440], P('col', 'row'), may hold values from -0.19921875 to 0.19921875
- pair_final: int32 [8, 4, 128], P('row', 'col'), may hold values from 0 to 31
- pair_initial: int32 [8, 4, 128], P('row', 'col'), may hold values from 0 to 31
- map_final: int32 [8, 32, 440], P('row', 'col'), may hold values from 0 to 439, each once within a row
- map_initial: int32 [4, 32, 440], P('col', 'row'), may hold values from 0 to 439, each once within a row
- counts: int32 [8, 4], P('row', 'col'), may hold values from 16 to 128, as said below
Outputs:
- density: float32 [440, 440], replicated
Inputs may be any that keep to these rules, and one draw needn't show every extreme that they name: `counts`: slots at or past a cell's count are ignored. Exactly one cell of every draw has 128 live slots.
All inputs are finite; a program needn't handle non-finite values.
Results may differ from a plain program's by a relative error of at most 0.0003.
Values may be sent and summed in bfloat16 or wider, within the bound.
A program may use at most 64 MiB of HBM per device.

v0:
```python
import jax
import jax.numpy as jnp
from jax import lax
from jax.sharding import PartitionSpec as P

GROUP = 32


def permute_columns(blocks, orbital_map):
    return jnp.take(blocks, orbital_map, axis=1)


def shards(final_amp, initial_amp, pair_final, pair_initial, map_final, map_initial, counts):
    own_final = jax.vmap(permute_columns)(final_amp[0], map_final[0])[None]
    own_initial = jax.vmap(permute_columns)(initial_amp[0], map_initial[0])[None]
    row_seg = lax.all_gather(own_final, "col", axis=1, tiled=True)[0]
    column_seg = lax.all_gather(own_initial, "row", axis=1, tiled=True)[0]
    slots_final = pair_final[0, 0]
    slots_initial = pair_initial[0, 0]
    live_count = counts[0, 0]
    orbitals = final_amp.shape[3]
    group_size = GROUP

    def advance(index, summed):
        first_slot = index * group_size
        which_final = lax.dynamic_slice_in_dim(slots_final, first_slot, group_size)
        which_initial = lax.dynamic_slice_in_dim(slots_initial, first_slot, group_size)
        live_mask = first_slot + jnp.arange(group_size, dtype=jnp.int32) < live_count
        left = jnp.take(row_seg, which_final, axis=0)
        right = jnp.take(column_seg, which_initial, axis=0)
        left = jnp.where(live_mask[:, None, None], left, jnp.zeros_like(left))
        product = lax.dot_general(
            left.reshape(-1, orbitals),
            right.reshape(-1, orbitals),
            (((0,), (0,)), ((), ())),
            preferred_element_type=jnp.float32,
        )
        return summed + product

    turns = (live_count + group_size - 1) // group_size
    partial_density = lax.fori_loop(0, turns, advance, jnp.zeros((orbitals, orbitals), jnp.float32))
    band = lax.psum_scatter(partial_density, "col", scatter_dimension=0, tiled=True)
    band = lax.psum(band, "row")
    density = lax.all_gather(band, "col", axis=0, tiled=True)
    return density


def solution(mesh):
    placed = (
        P("row", "col", None, None),
        P("col", "row", None, None),
        P("row", "col", None),
        P("row", "col", None),
        P("row", "col", None),
        P("col", "row", None),
        P("row", "col"),
    )
    return jax.shard_map(shards, mesh=mesh, in_specs=placed, out_specs=P(), check_vma=False)
```

profile of v0, /device:TPU:0, one launch (start us, length us, event | category | flops | bytes accessed | tf_op | source)
XLA Modules:
  0.0 321.1 jit_solution(12124861493017973160)
XLA Ops:
  6.5 0.0 copy-start
  6.5 0.0 all-gather.4.cloned.1.call-start
  6.5 0.8 fusion.18
  7.3 0.7 compare_and_fusion.2
  8.1 0.1 reshape.110
  8.2 0.0 copy-done
  8.2 0.0 copy-start.2
  8.2 0.0 copy-start.1
  8.2 30.8 %gather_fusion.2 = bf16[3520,128]{1,0:T(8,128)(2,1)S(1)} fusion(bf16[8,128,440]{1,2,0:T(8,128)(2,1)S(1)} %bitcast.44, s32[3520]{0:T(1024)S(1)} %reshape.110), kind=kCustom, calls=%fused_computation.2 | custom fusion | bytes 1830400 | tf_op jit(solution)/shard_map/vmap(jit(_take))/gather | solution.py:10
  39.0 1.4 broadcast_select_fusion
  40.4 0.0 all-gather.4.cloned.1.call-update
  40.4 0.0 all-gather.6.cloned.1.call-start
  40.4 0.0 copy-done.2
  40.5 0.1 reshape.116
  40.5 0.0 copy-done.1
  40.5 15.7 %gather_fusion.3 = bf16[1760,128]{1,0:T(8,128)(2,1)S(1)} fusion(bf16[4,128,440]{1,2,0:T(8,128)(2,1)S(1)} %bitcast.45, s32[1760]{0:T(1024)S(1)} %reshape.116), kind=kCustom, calls=%fused_computation.3 | custom fusion | bytes 915200 | tf_op jit(solution)/shard_map/vmap(jit(_take))/gather | solution.py:10
  56.3 1.1 broadcast_select_fusion.1
  57.4 0.0 all-gather.6.cloned.1.call-update
  57.4 0.0 all-reduce.4.cloned.1.call-start
  58.2 56.1 %all-gather.4.cloned.1.call-done = bf16[1,32,128,440]{2,3,0,1:T(8,128)(2,1)} async-done(((bf16[1,8,128,440]{2,3,0,1:T(8,128)(2,1)}), bf16[1,32,128,440]{2,3,0,1:T(8,128)(2,1)}) %all-gather.4.cloned.1.call-update) | async-done | bytes 3604496 | tf_op jit(solution)/shard_map/all_gather | solution.py:16
  114.3 6.4 %copy.18 = bf16[32,128,440]{2,1,0:T(8,128)(2,1)} copy(bf16[32,128,440]{1,2,0:T(8,128)(2,1)} %bitcast.47) | data formatting | bytes 7208960 | tf_op jit(solution)/shard_map/while | solution.py:41
  120.7 28.2 %all-gather.6.cloned.1.call-done = bf16[1,32,128,440]{2,3,0,1:T(8,128)(2,1)} async-done(((bf16[1,4,128,440]{2,3,0,1:T(8,128)(2,1)}), bf16[1,32,128,440]{2,3,0,1:T(8,128)(2,1)}) %all-gather.6.cloned.1.call-update) | async-done | bytes 3604496 | tf_op jit(solution)/shard_map/all_gather | solution.py:17
  148.9 0.0 copy-start.3
  148.9 0.0 copy-start.4
  148.9 6.5 %copy.19 = bf16[32,128,440]{2,1,0:T(8,128)(2,1)} copy(bf16[32,128,440]{1,2,0:T(8,128)(2,1)} %bitcast.48) | data formatting | bytes 7208960 | tf_op jit(solution)/shard_map/while | solution.py:41
  155.3 0.1 broadcast_in_dim.43
  155.4 0.0 copy-done.3
  155.5 0.0 copy-done.4
  155.5 0.0 copy-start.5
  155.5 33.5 %while.10 = (s32[]{:T(128)}, f32[440,440]{1,0:T(8,128)S(1)}, s32[]{:T(128)}, s32[]{:T(128)}, s32[128]{0:T(128)S(1)}, /*index=5*/bf16[32,128,440]{2,1,0:T(8,128)(...) while((s32[]{:T(128)}, f32[440,440]{1,0:T(8,128)S(1)}, ...), condition=%wide.region_1.3_spmd, body=%wide.region_0.0_spmd.sunk | while | flops 1591574016 | bytes 23185264 | solution.py:41
  155.5 0.1 compare_and_fusion.5
  155.6 5.0 %gather_fusion = bf16[32,128,440]{2,1,0:T(8,128)(2,1)} fusion(bf16[32,128,440]{2,1,0:T(8,128)(2,1)} %get-tuple-element.169, s32[1024]{0:T(1024)S(1)} %pad_clamp_fusion.4), kind=kCustom, calls=%fused_computation.1.clone.clone.1 | custom fusion | bytes 7209088 | tf_op jit(solution)/shard_map/while/body/jit(_take)/gather | solution.py:30
  160.6 4.9 %gather_fusion.1 = bf16[32,128,440]{2,1,0:T(8,128)(2,1)} fusion(bf16[32,128,440]{2,1,0:T(8,128)(2,1)} %get-tuple-element.167, s32[1024]{0:T(1024)S(1)} %pad_clamp_fusion.5), kind=kCustom, calls=%fused_computation.clone.clone.1 | custom fusion | bytes 7209088 | tf_op jit(solution)/shard_map/while/body/jit(_take)/gather | solution.py:29
  165.5 0.7 add_compare_fusion.2
  166.1 6.1 %fusion.25 = f32[440,440]{1,0:T(8,128)S(1)} fusion(f32[440,440]{1,0:T(8,128)S(1)} %get-tuple-element.151, bf16[32,128,440]{2,1,0:T(8,128)(2,1)} %gather_fusion, pred[32]{0:T(512)(128)(4,1)S(1)} %get-tuple-element.135, bf16[32,128,440]{2,1,0:T(8,128)(2,1)} %gather_fusion.1, pred[32]{0:T(512)(128)(4,1)S(1)} %get-tuple-element.137, ...), kind=kOutput, calls=%fused_computation.13.clone.1 | convolution fusion | flops 1591571456 | bytes 8757856 | tf_op jit(solution)/shard_map/while/body/dot_general | solution.py:32
  172.2 0.1 compare_and_fusion.5
  172.3 5.0 %gather_fusion = bf16[32,128,440]{2,1,0:T(8,128)(2,1)} fusion(bf16[32,128,440]{2,1,0:T(8,128)(2,1)} %get-tuple-element.169, s32[1024]{0:T(1024)S(1)} %pad_clamp_fusion.4), kind=kCustom, calls=%fused_computation.1.clone.clone.1 | custom fusion | bytes 7209088 | tf_op jit(solution)/shard_map/while/body/jit(_take)/gather | solution.py:30
  177.3 4.9 %gather_fusion.1 = bf16[32,128,440]{2,1,0:T(8,128)(2,1)} fusion(bf16[32,128,440]{2,1,0:T(8,128)(2,1)} %get-tuple-element.167, s32[1024]{0:T(1024)S(1)} %pad_clamp_fusion.5), kind=kCustom, calls=%fused_computation.clone.clone.1 | custom fusion | bytes 7209088 | tf_op jit(solution)/shard_map/while/body/jit(_take)/gather | solution.py:29
  182.2 0.7 add_compare_fusion.2
  182.9 6.1 %fusion.25 = f32[440,440]{1,0:T(8,128)S(1)} fusion(f32[440,440]{1,0:T(8,128)S(1)} %get-tuple-element.151, bf16[32,128,440]{2,1,0:T(8,128)(2,1)} %gather_fusion, pred[32]{0:T(512)(128)(4,1)S(1)} %get-tuple-element.135, bf16[32,128,440]{2,1,0:T(8,128)(2,1)} %gather_fusion.1, pred[32]{0:T(512)(128)(4,1)S(1)} %get-tuple-element.137, ...), kind=kOutput, calls=%fused_computation.13.clone.1 | convolution fusion | flops 1591571456 | bytes 8757856 | tf_op jit(solution)/shard_map/while/body/dot_general | solution.py:32
  188.9 22.8 %fusion = f32[112,440]{1,0:T(8,128)S(1)} fusion(f32[440,440]{1,0:T(8,128)S(1)} %get-tuple-element.49), kind=kCustom, calls=%all-reduce-scatter | all-reduce-scatter fusion | flops 197121 | bytes 972032
  211.7 2.1 collective-permute-start
  213.9 0.0 copy-done.5
  213.9 0.6 dynamic-slice.4
  215.1 0.2 collective-permute-done
  215.3 0.2 concatenate.6
  215.6 0.7 constant_dynamic-slice_fusion
  216.3 0.0 all-reduce.4.cloned.1.call-update
  216.3 74.9 %all-reduce.4.cloned.1.call-done = f32[110,440]{1,0:T(8,128)} async-done(((f32[110,440]{1,0:T(8,128)}), f32[110,440]{1,0:T(8,128)}) %all-reduce.4.cloned.1.call-update) | async-done | bytes 193616 | tf_op jit(solution)/shard_map/psum | solution.py:43
  291.2 1.1 copy.20
  292.3 20.9 %all-gather = f32[4,110,440]{1,2,0:T(8,128)S(1)} all-gather(f32[1,110,440]{1,2,0:T(8,128)S(1)} %copy.20), channel_id=1, replica_groups=mesh['row'=8,'col'=4] {'col'}, dimensions={0}, use_global_device_ids=true | all-gather | bytes 968000 | tf_op jit(solution)/shard_map/all_gather | solution.py:44
  313.2 0.4 copy.21
  313.6 1.0 reshape.125
  (7 shorter events, 0.0 us)
Async XLA Ops:
  6.5 1.6 copy-start
  6.5 107.7 %all-gather.4.cloned.1.call-start = ((), (), s32[]{:S(2)}) async-start(), calls=%async_computation | async-start | bytes 4505600 | tf_op jit(solution)/shard_map/all_gather | solution.py:16
  8.2 32.3 %copy-start.2 = (s32[1,4,440]{2,1,0:T(4,128)S(1)}, s32[1,4,440]{2,1,0:T(4,128)}, u32[]{:S(2)}) copy-start(s32[1,4,440]{2,1,0:T(4,128)} %param.16) | copy-start | bytes 21124
  8.2 32.4 %copy-start.1 = (bf16[1,4,128,440]{2,3,1,0:T(8,128)(2,1)S(1)}, bf16[1,4,128,440]{2,3,1,0:T(8,128)(2,1)}, u32[]{:S(2)}) copy-start(bf16[1,4,128,440]{2,3,1,0:T(8,128)(2,1)} %param.12) | copy-start | bytes 1351684
  40.4 108.5 %all-gather.6.cloned.1.call-start = ((), (), s32[]{:S(2)}) async-start(), calls=%async_computation.1 | async-start | bytes 4055040 | tf_op jit(solution)/shard_map/all_gather | solution.py:17
  57.4 233.8 %all-reduce.4.cloned.1.call-start = ((), (), s32[]{:S(2)}) async-start(), calls=%async_computation.2 | async-start | bytes 458752 | tf_op jit(solution)/shard_map/psum | solution.py:43
  148.9 6.6 %copy-start.3 = (s32[1,1,128]{2,1,0:T(1,128)S(1)}, s32[1,1,128]{2,1,0:T(1,128)}, u32[]{:S(2)}) copy-start(s32[1,1,128]{2,1,0:T(1,128)} %param.13) | copy-start | bytes 1540
  148.9 6.6 %copy-start.4 = (s32[1,1,128]{2,1,0:T(1,128)S(1)}, s32[1,1,128]{2,1,0:T(1,128)}, u32[]{:S(2)}) copy-start(s32[1,1,128]{2,1,0:T(1,128)} %param.14) | copy-start | bytes 1540
  155.5 58.4 %copy-start.5 = (u32[32]{0:T(128)S(1)}, u32[32]{0:T(128)}, u32[]{:S(2)}) copy-start(u32[32]{0:T(128)} %constant.104) | copy-start | bytes 388
  211.7 3.6 %collective-permute-start = (f32[6,440]{1,0:T(8,128)S(1)}, f32[6,440]{1,0:T(8,128)S(1)}, u32[]{:S(2)}, u32[]{:S(2)}) collective-permute-start(f32[6,440]{1,0:T(8,128)S(1)} %slice.8), channel_id=1, source_target_pairs={{0,1},{1,2},{2,3},{4,5},{5,6},{6,7},{8,9},{9,10},{10,11},{12,13},{... | collective-permute-start | bytes 31688
Sparse Core Ops, SparseCore 0:
  40.5 73.7 all-gather.3
  116.2 32.6 all-gather.5
  216.4 74.7 all-reduce.3
where the time goes:
time: 322 us; the launch traced here: 321 us
  waiting for transfers between devices  159 us (49%)
  local copies, waits for them, and re-layouts  83.4 us (26%)
  blocking collectives  43.7 us (14%)
  between operations  14.6 us (5%)
  matrix products  12.1 us (4%)
  other arithmetic  5.57 us (2%)
    psum x1, waiting for transfers between devices, shards(): band = lax.psum(band, 'row')  74.9 us
    all_gather x1, waiting for transfers between devices, shards(): row_seg = lax.all_gather(own_final, 'col', axis=1, tiled=True)[0]  56.1 us
    gather x4, local copies, waits for them, and re-layouts, permute_columns(): return jnp.take(blocks, orbital_map, axis=1)  46.6 us
    all_gather x1, waiting for transfers between devices, shards(): column_seg = lax.all_gather(own_initial, 'row', axis=1, tiled=True)[0]  28.2 us
    unnamed x1, blocking collectives  22.8 us
    all_gather x1, blocking collectives, shards(): density = lax.all_gather(band, 'col', axis=0, tiled=True)  20.9 us
    while x2, local copies, waits for them, and re-layouts, shards(): lax.fori_loop(0, turns, advance, jnp.zeros((orbitals, orbitals), jnp.floa...  12.9 us
    dot_general x2, matrix products, advance(): lax.dot_general(left.reshape(-1, orbitals), right.reshape(-1, orbitals),...  12.1 us
  transfers between devices with their start and end apart: 4, of which 4 were waited for; matrix products, arithmetic and copies ran while one was open for 7% of the time, Pallas kernels for 0%

commit v1 on v0

--- a/solution.py
+++ b/solution.py
@@ -41,7 +41,8 @@
     partial_density = lax.fori_loop(0, turns, advance, jnp.zeros((orbitals, orbitals), jnp.float32))
     band = lax.psum_scatter(partial_density, "col", scatter_dimension=0, tiled=True)
     band = lax.psum(band, "row")
-    density = lax.all_gather(band, "col", axis=0, tiled=True)
+    sent = jnp.stack([band] * lax.axis_size("col"))
+    density = jnp.concatenate(lax.all_to_all(sent, "col", 0, 0), axis=0)
     return density
 
 

time: 322 us -> 329 us (1.022)
  blocking collectives: 43.7 us -> 50.4 us
    all_to_all x0 -> x1, blocking collectives: none -> 27.6 us  [shards(): density = jnp.concatenate(lax.all_to_all(sent, 'col', 0, 0), axis=0)]
    all_gather x1 -> x0, blocking collectives: 20.9 us -> none  [shards(): density = lax.all_gather(band, 'col', axis=0, tiled=True)]
where the time goes in v1:
time: 329 us; the launch traced here: 328 us
  waiting for transfers between devices  159 us (48%)
  local copies, waits for them, and re-layouts  83.5 us (25%)
  blocking collectives  50.4 us (15%)
  between operations  14.6 us (4%)
  matrix products  12.1 us (4%)
  other arithmetic  5.57 us (2%)
    psum x1, waiting for transfers between devices, shards(): band = lax.psum(band, 'row')  74.9 us
    all_gather x1, waiting for transfers between devices, shards(): row_seg = lax.all_gather(own_final, 'col', axis=1, tiled=True)[0]  56.1 us
    gather x4, local copies, waits for them, and re-layouts, permute_columns(): return jnp.take(blocks, orbital_map, axis=1)  46.6 us
    all_gather x1, waiting for transfers between devices, shards(): column_seg = lax.all_gather(own_initial, 'row', axis=1, tiled=True)[0]  28.2 us
    all_to_all x1, blocking collectives, shards(): density = jnp.concatenate(lax.all_to_all(sent, 'col', 0, 0), axis=0)  27.6 us
    unnamed x1, blocking collectives  22.8 us
    while x2, local copies, waits for them, and re-layouts, shards(): lax.fori_loop(0, turns, advance, jnp.zeros((orbitals, orbitals), jnp.floa...  12.9 us
    dot_general x2, matrix products, advance(): lax.dot_general(left.reshape(-1, orbitals), right.reshape(-1, orbitals),...  12.1 us
  transfers between devices with their start and end apart: 4, of which 4 were waited for; matrix products, arithmetic and copies ran while one was open for 7% of the time, Pallas kernels for 0%

profile of v1, /device:TPU:0, one launch (start us, length us, event | category | flops | bytes accessed | tf_op | source)
XLA Modules:
  0.0 327.8 jit_solution(6601023183896258490)
XLA Ops:
  6.5 0.0 copy-start
  6.5 0.0 all-gather.3.cloned.1.call-start
  6.5 0.8 fusion.18
  7.3 0.7 compare_and_fusion.2
  8.1 0.1 reshape.116
  8.2 0.0 copy-done
  8.2 0.0 copy-start.2
  8.2 0.0 copy-start.1
  8.2 30.8 %gather_fusion.2 = bf16[3520,128]{1,0:T(8,128)(2,1)S(1)} fusion(bf16[8,128,440]{1,2,0:T(8,128)(2,1)S(1)} %bitcast.43, s32[3520]{0:T(1024)S(1)} %reshape.116), kind=kCustom, calls=%fused_computation.2 | custom fusion | bytes 1830400 | tf_op jit(solution)/shard_map/vmap(jit(_take))/gather | solution.py:10
  39.0 1.4 broadcast_select_fusion
  40.4 0.0 all-gather.3.cloned.1.call-update
  40.4 0.0 all-gather.5.cloned.1.call-start
  40.4 0.0 copy-done.2
  40.5 0.1 reshape.122
  40.5 0.0 copy-done.1
  40.5 15.7 %gather_fusion.3 = bf16[1760,128]{1,0:T(8,128)(2,1)S(1)} fusion(bf16[4,128,440]{1,2,0:T(8,128)(2,1)S(1)} %bitcast.44, s32[1760]{0:T(1024)S(1)} %reshape.122), kind=kCustom, calls=%fused_computation.3 | custom fusion | bytes 915200 | tf_op jit(solution)/shard_map/vmap(jit(_take))/gather | solution.py:10
  56.3 1.1 broadcast_select_fusion.1
  57.4 0.0 all-gather.5.cloned.1.call-update
  57.4 0.0 all-reduce.4.cloned.1.call-start
  58.2 56.1 %all-gather.3.cloned.1.call-done = bf16[1,32,128,440]{2,3,0,1:T(8,128)(2,1)} async-done(((bf16[1,8,128,440]{2,3,0,1:T(8,128)(2,1)}), bf16[1,32,128,440]{2,3,0,1:T(8,128)(2,1)}) %all-gather.3.cloned.1.call-update) | async-done | bytes 3604496 | tf_op jit(solution)/shard_map/all_gather | solution.py:16
  114.3 6.4 %copy.18 = bf16[32,128,440]{2,1,0:T(8,128)(2,1)} copy(bf16[32,128,440]{1,2,0:T(8,128)(2,1)} %bitcast.46) | data formatting | bytes 7208960 | tf_op jit(solution)/shard_map/while | solution.py:41
  120.7 28.2 %all-gather.5.cloned.1.call-done = bf16[1,32,128,440]{2,3,0,1:T(8,128)(2,1)} async-done(((bf16[1,4,128,440]{2,3,0,1:T(8,128)(2,1)}), bf16[1,32,128,440]{2,3,0,1:T(8,128)(2,1)}) %all-gather.5.cloned.1.call-update) | async-done | bytes 3604496 | tf_op jit(solution)/shard_map/all_gather | solution.py:17
  148.9 0.0 copy-start.3
  148.9 0.0 copy-start.4
  148.9 6.5 %copy.19 = bf16[32,128,440]{2,1,0:T(8,128)(2,1)} copy(bf16[32,128,440]{1,2,0:T(8,128)(2,1)} %bitcast.47) | data formatting | bytes 7208960 | tf_op jit(solution)/shard_map/while | solution.py:41
  155.3 0.1 broadcast_in_dim.43
  155.4 0.0 copy-done.3
  155.5 0.0 copy-done.4
  155.5 0.0 copy-start.5
  155.5 33.5 %while.10 = (s32[]{:T(128)}, f32[440,440]{1,0:T(8,128)S(1)}, s32[]{:T(128)}, s32[]{:T(128)}, s32[128]{0:T(128)S(1)}, /*index=5*/bf16[32,128,440]{2,1,0:T(8,128)(...) while((s32[]{:T(128)}, f32[440,440]{1,0:T(8,128)S(1)}, ...), condition=%wide.region_1.3_spmd, body=%wide.region_0.0_spmd.sunk | while | flops 1591574016 | bytes 23185264 | solution.py:41
  155.5 0.1 compare_and_fusion.5
  155.6 5.0 %gather_fusion = bf16[32,128,440]{2,1,0:T(8,128)(2,1)} fusion(bf16[32,128,440]{2,1,0:T(8,128)(2,1)} %get-tuple-element.169, s32[1024]{0:T(1024)S(1)} %pad_clamp_fusion.4), kind=kCustom, calls=%fused_computation.1.clone.clone.1 | custom fusion | bytes 7209088 | tf_op jit(solution)/shard_map/while/body/jit(_take)/gather | solution.py:30
  160.6 4.9 %gather_fusion.1 = bf16[32,128,440]{2,1,0:T(8,128)(2,1)} fusion(bf16[32,128,440]{2,1,0:T(8,128)(2,1)} %get-tuple-element.167, s32[1024]{0:T(1024)S(1)} %pad_clamp_fusion.5), kind=kCustom, calls=%fused_computation.clone.clone.1 | custom fusion | bytes 7209088 | tf_op jit(solution)/shard_map/while/body/jit(_take)/gather | solution.py:29
  165.5 0.7 add_compare_fusion.2
  166.1 6.1 %fusion.25 = f32[440,440]{1,0:T(8,128)S(1)} fusion(f32[440,440]{1,0:T(8,128)S(1)} %get-tuple-element.151, bf16[32,128,440]{2,1,0:T(8,128)(2,1)} %gather_fusion, pred[32]{0:T(512)(128)(4,1)S(1)} %get-tuple-element.135, bf16[32,128,440]{2,1,0:T(8,128)(2,1)} %gather_fusion.1, pred[32]{0:T(512)(128)(4,1)S(1)} %get-tuple-element.137, ...), kind=kOutput, calls=%fused_computation.13.clone.1 | convolution fusion | flops 1591571456 | bytes 8757856 | tf_op jit(solution)/shard_map/while/body/dot_general | solution.py:32
  172.2 0.1 compare_and_fusion.5
  172.3 5.0 %gather_fusion = bf16[32,128,440]{2,1,0:T(8,128)(2,1)} fusion(bf16[32,128,440]{2,1,0:T(8,128)(2,1)} %get-tuple-element.169, s32[1024]{0:T(1024)S(1)} %pad_clamp_fusion.4), kind=kCustom, calls=%fused_computation.1.clone.clone.1 | custom fusion | bytes 7209088 | tf_op jit(solution)/shard_map/while/body/jit(_take)/gather | solution.py:30
  177.3 4.9 %gather_fusion.1 = bf16[32,128,440]{2,1,0:T(8,128)(2,1)} fusion(bf16[32,128,440]{2,1,0:T(8,128)(2,1)} %get-tuple-element.167, s32[1024]{0:T(1024)S(1)} %pad_clamp_fusion.5), kind=kCustom, calls=%fused_computation.clone.clone.1 | custom fusion | bytes 7209088 | tf_op jit(solution)/shard_map/while/body/jit(_take)/gather | solution.py:29
  182.2 0.7 add_compare_fusion.2
  182.9 6.1 %fusion.25 = f32[440,440]{1,0:T(8,128)S(1)} fusion(f32[440,440]{1,0:T(8,128)S(1)} %get-tuple-element.151, bf16[32,128,440]{2,1,0:T(8,128)(2,1)} %gather_fusion, pred[32]{0:T(512)(128)(4,1)S(1)} %get-tuple-element.135, bf16[32,128,440]{2,1,0:T(8,128)(2,1)} %gather_fusion.1, pred[32]{0:T(512)(128)(4,1)S(1)} %get-tuple-element.137, ...), kind=kOutput, calls=%fused_computation.13.clone.1 | convolution fusion | flops 1591571456 | bytes 8757856 | tf_op jit(solution)/shard_map/while/body/dot_general | solution.py:32
  188.9 22.8 %fusion = f32[112,440]{1,0:T(8,128)S(1)} fusion(f32[440,440]{1,0:T(8,128)S(1)} %get-tuple-element.49), kind=kCustom, calls=%all-reduce-scatter | all-reduce-scatter fusion | flops 197121 | bytes 972032
  211.7 2.1 collective-permute-start
  213.9 0.0 copy-done.5
  213.9 0.6 dynamic-slice.4
  215.1 0.2 collective-permute-done
  215.3 0.2 concatenate.6
  215.6 0.7 constant_dynamic-slice_fusion
  216.3 0.0 all-reduce.4.cloned.1.call-update
  216.3 74.9 %all-reduce.4.cloned.1.call-done = f32[110,440]{1,0:T(8,128)} async-done(((f32[110,440]{1,0:T(8,128)}), f32[110,440]{1,0:T(8,128)}) %all-reduce.4.cloned.1.call-update) | async-done | bytes 193616 | tf_op jit(solution)/shard_map/psum | solution.py:43
  291.2 1.1 copy.20
  292.3 0.1 stack.2
  292.3 27.6 %all_to_all.5 = f32[4,110,440]{1,2,0:T(8,128)S(1)} all-to-all(f32[4,110,440]{1,2,0:T(8,128)S(1)} %stack.2), channel_id=1, replica_groups=mesh['row'=8,'col'=4] {'col'}, dimensions={0} | all-to-all | bytes 1548800 | tf_op jit(solution)/shard_map/all_to_all | solution.py:45
  319.9 0.4 copy.21
  320.3 1.0 reshape.99
  (7 shorter events, 0.0 us)
Async XLA Ops:
  6.5 1.6 copy-start
  6.5 107.7 %all-gather.3.cloned.1.call-start = ((), (), s32[]{:S(2)}) async-start(), calls=%async_computation.1 | async-start | bytes 4505600 | tf_op jit(solution)/shard_map/all_gather | solution.py:16
  8.2 32.3 %copy-start.2 = (s32[1,4,440]{2,1,0:T(4,128)S(1)}, s32[1,4,440]{2,1,0:T(4,128)}, u32[]{:S(2)}) copy-start(s32[1,4,440]{2,1,0:T(4,128)} %param.16) | copy-start | bytes 21124
  8.2 32.4 %copy-start.1 = (bf16[1,4,128,440]{2,3,1,0:T(8,128)(2,1)S(1)}, bf16[1,4,128,440]{2,3,1,0:T(8,128)(2,1)}, u32[]{:S(2)}) copy-start(bf16[1,4,128,440]{2,3,1,0:T(8,128)(2,1)} %param.12) | copy-start | bytes 1351684
  40.4 108.5 %all-gather.5.cloned.1.call-start = ((), (), s32[]{:S(2)}) async-start(), calls=%async_computation.2 | async-start | bytes 4055040 | tf_op jit(solution)/shard_map/all_gather | solution.py:17
  57.4 233.8 %all-reduce.4.cloned.1.call-start = ((), (), s32[]{:S(2)}) async-start(), calls=%async_computation.3 | async-start | bytes 458752 | tf_op jit(solution)/shard_map/psum | solution.py:43
  148.9 6.6 %copy-start.3 = (s32[1,1,128]{2,1,0:T(1,128)S(1)}, s32[1,1,128]{2,1,0:T(1,128)}, u32[]{:S(2)}) copy-start(s32[1,1,128]{2,1,0:T(1,128)} %param.13) | copy-start | bytes 1540
  148.9 6.6 %copy-start.4 = (s32[1,1,128]{2,1,0:T(1,128)S(1)}, s32[1,1,128]{2,1,0:T(1,128)}, u32[]{:S(2)}) copy-start(s32[1,1,128]{2,1,0:T(1,128)} %param.14) | copy-start | bytes 1540
  155.5 58.4 %copy-start.5 = (u32[32]{0:T(128)S(1)}, u32[32]{0:T(128)}, u32[]{:S(2)}) copy-start(u32[32]{0:T(128)} %constant.104) | copy-start | bytes 388
  211.7 3.6 %collective-permute-start = (f32[6,440]{1,0:T(8,128)S(1)}, f32[6,440]{1,0:T(8,128)S(1)}, u32[]{:S(2)}, u32[]{:S(2)}) collective-permute-start(f32[6,440]{1,0:T(8,128)S(1)} %slice.8), channel_id=1, source_target_pairs={{0,1},{1,2},{2,3},{4,5},{5,6},{6,7},{8,9},{9,10},{10,11},{12,13},{... | collective-permute-start | bytes 31688
Sparse Core Ops, SparseCore 0:
  40.5 73.7 all-gather.2
  116.2 32.6 all-gather.4
  216.4 74.7 all-reduce.3
